TPU v7x, 32 devices: a whole 2x2x4 slice. The times are simulated.
32 devices in a mesh: dp: 8 (over z, core), chan: 4 (over y, x).
Axes of the slice: x: 2, y: 2, z: 4, core: 2. Of those that a mesh axis runs over, the one named last changes fastest.
Arguments:
- images: bfloat16 [16, 16, 16, 2816], P('dp', None, None, 'chan'), may hold values from -6 to 6
- kernel: float32 [7, 7, 2816], P(None, None, 'chan'), may hold values from -0.875 to 0.875
- layernorm_gain: float32 [2816], P('chan'), may hold values from 0.25 to 1.75
- layernorm_bias: float32 [2816], P('chan'), may hold values from -3 to 3
- w_expand: bfloat16 [2816, 11264], P('dp', 'chan'), may hold values from -0.109375 to 0.109375
- w_reduce: bfloat16 [11264, 2816], P('chan', 'dp'), may hold values from -0.0546875 to 0.0546875
- layer_scale: float32 [2816], P('chan'), may hold values from 0.25 to 1
- cotangent: bfloat16 [16, 16, 16, 2816], P('dp', None, None, 'chan'), may hold values from -6 to 6
Outputs:
- output: bfloat16 [16, 16, 16, 2816], P('dp', None, None, 'chan')
- grad_images: bfloat16 [16, 16, 16, 2816], P('dp', None, None, 'chan')
- grad_kernel: float32 [7, 7, 2816], P(None, None, 'chan')
- gain_gradient: float32 [2816], P('chan')
- grad_bias: float32 [2816], P('chan')
- grad_expand: float32 [2816, 11264], P('dp', 'chan')
- grad_reduce: float32 [11264, 2816], P('chan', 'dp')
- grad_scale: float32 [2816], P('chan')
All inputs are finite; a program needn't handle non-finite values.
Results may differ from a plain program's by a relative error of at most 0.025.
Values may be sent and summed in bfloat16 or wider, within the bound.
A program may use at most 128 MiB of HBM per device.

v0:
```python
import math
import jax
import jax.numpy as jnp
from jax import lax
from jax.sharding import PartitionSpec as P

eps = 1e-06


def depthwise(field, kern):
    height = field.shape[1]
    breadth = field.shape[2]
    padded = jnp.pad(field, ((0, 0), (3, 3), (3, 3), (0, 0)))
    total = jnp.zeros(field.shape, jnp.float32)
    for i in range(7):
        for j in range(7):
            total = total + padded[:, i : i + height, j : j + breadth, :] * kern[i, j]
    return total


def normal_cdf(value):
    return 0.5 * (1.0 + jax.scipy.special.erf(value / math.sqrt(2.0)))


def body(
    images, kernel, layernorm_gain, layernorm_bias, w_expand, w_reduce, layer_scale, cotangent
):
    shape_in = images.shape
    height = shape_in[1]
    breadth = shape_in[2]
    positions = shape_in[0] * height * breadth
    local_chan = shape_in[3]
    image_width = local_chan * lax.axis_size("chan")
    xf = images.astype(jnp.float32)
    conv = depthwise(xf, kernel).reshape(positions, local_chan)
    mean_val = lax.psum(jnp.sum(conv, axis=1), "chan")[:, None] / image_width
    centred_rows = conv - mean_val
    var = lax.psum(jnp.sum(centred_rows * centred_rows, axis=1), "chan")[:, None] / image_width
    inverse_deviation = lax.rsqrt(var + eps)
    standardized_input = centred_rows * inverse_deviation
    normed_output = (standardized_input * layernorm_gain + layernorm_bias).astype(jnp.bfloat16)
    normed_all = lax.all_gather(normed_output, "chan", axis=1, tiled=True)
    expand_all = lax.all_gather(w_expand, "dp", axis=0, tiled=True)
    pre = jnp.dot(normed_all, expand_all, preferred_element_type=jnp.float32)
    hidden = (pre * normal_cdf(pre)).astype(jnp.bfloat16)
    reduce_all = lax.all_gather(w_reduce, "dp", axis=1, tiled=True)
    partial_branch = jnp.dot(hidden, reduce_all, preferred_element_type=jnp.float32)
    branch = lax.psum_scatter(
        partial_branch.astype(jnp.bfloat16), "chan", scatter_dimension=1, tiled=True
    ).astype(jnp.float32)
    xr = xf.reshape(positions, local_chan)
    output = (xr + layer_scale * branch).astype(jnp.bfloat16).reshape(shape_in)
    dyf = cotangent.astype(jnp.float32).reshape(positions, local_chan)
    scale_part = jnp.sum(dyf * branch, axis=0)
    dbranch = (dyf * layer_scale).astype(jnp.bfloat16)
    dbranch_all = lax.all_gather(dbranch, "chan", axis=1, tiled=True)
    dhidden = lax.dot_general(
        dbranch_all, reduce_all, (((1,), (1,)), ((), ())), preferred_element_type=jnp.float32
    )
    slope = normal_cdf(pre) + pre * jnp.exp(-0.5 * pre * pre) / math.sqrt(2.0 * math.pi)
    dpre = (dhidden * slope).astype(jnp.bfloat16)
    columns = normed_all
    grad_expand = lax.psum_scatter(
        lax.dot_general(
            columns, dpre, (((0,), (0,)), ((), ())), preferred_element_type=jnp.float32
        ).astype(jnp.bfloat16),
        "dp",
        scatter_dimension=0,
        tiled=True,
    ).astype(jnp.float32)
    partial_normed = lax.dot_general(
        dpre, expand_all, (((1,), (1,)), ((), ())), preferred_element_type=jnp.float32
    )
    normed_grad = lax.psum_scatter(
        partial_normed.astype(jnp.bfloat16), "chan", scatter_dimension=1, tiled=True
    ).astype(jnp.float32)
    columns = dbranch_all
    grad_reduce = (
        lax.psum_scatter(
            lax.dot_general(
                columns, hidden, (((0,), (0,)), ((), ())), preferred_element_type=jnp.float32
            ).astype(jnp.bfloat16),
            "dp",
            scatter_dimension=0,
            tiled=True,
        )
        .astype(jnp.float32)
        .T
    )
    gain_partial = jnp.sum(normed_grad * standardized_input, axis=0)
    bias_part = jnp.sum(normed_grad, axis=0)
    standardized_grad = normed_grad * layernorm_gain
    first_half, second_half = lax.psum(
        (
            jnp.sum(standardized_grad, axis=1),
            jnp.sum(standardized_grad * standardized_input, axis=1),
        ),
        "chan",
    )
    conv_output_grad = inverse_deviation * (
        standardized_grad
        - first_half[:, None] / image_width
        - standardized_input * (second_half[:, None] / image_width)
    )
    conv_output_grad = conv_output_grad.reshape(shape_in)
    padded = jnp.pad(xf, ((0, 0), (3, 3), (3, 3), (0, 0)))
    dpad = jnp.pad(conv_output_grad, ((0, 0), (3, 3), (3, 3), (0, 0)))
    back = cotangent.astype(jnp.float32)
    kern_rows = []
    for i in range(7):
        tap_row = []
        for j in range(7):
            tap_row.append(
                jnp.sum(
                    padded[:, i : i + height, j : j + breadth, :] * conv_output_grad, axis=(0, 1, 2)
                )
            )
            back = back + dpad[:, 6 - i : 6 - i + height, 6 - j : 6 - j + breadth, :] * kernel[i, j]
        kern_rows.append(jnp.stack(tap_row))
    kernel_part = jnp.stack(kern_rows)
    grad_images = back.astype(jnp.bfloat16)
    grad_kernel, gain_gradient, grad_bias, grad_scale = (
        lax.psum(kernel_part.astype(jnp.bfloat16), "dp").astype(jnp.float32),
        lax.psum(gain_partial.astype(jnp.bfloat16), "dp").astype(jnp.float32),
        lax.psum(bias_part.astype(jnp.bfloat16), "dp").astype(jnp.float32),
        lax.psum(scale_part.astype(jnp.bfloat16), "dp").astype(jnp.float32),
    )
    return (
        output,
        grad_images,
        grad_kernel,
        gain_gradient,
        grad_bias,
        grad_expand,
        grad_reduce,
        grad_scale,
    )


def solution(mesh):
    in_specs = (
        P("dp", None, None, "chan"),
        P(None, None, "chan"),
        P("chan"),
        P("chan"),
        P("dp", "chan"),
        P("chan", "dp"),
        P("chan"),
        P("dp", None, None, "chan"),
    )
    out_specs = (
        P("dp", None, None, "chan"),
        P("dp", None, None, "chan"),
        P(None, None, "chan"),
        P("chan"),
        P("chan"),
        P("dp", "chan"),
        P("chan", "dp"),
        P("chan"),
    )
    return jax.shard_map(body, mesh=mesh, in_specs=in_specs, out_specs=out_specs, check_vma=False)
```

profile of v0, /device:TPU:0, one launch (start us, length us, event | category | flops | bytes accessed | tf_op | source)
XLA Modules:
  0.0 969.2 jit_solution(17701858807250672959)
XLA Ops:
  12.5 12.3 %fusion.114 = (f32[2,16,16]{2,1,0:T(8,128)S(1)}, f32[2,16,16,704]{3,2,1,0:T(8,128)S(1)}) fusion(f32[704]{0:T(1024)S(1)} %get-tuple-element.115, f32[704]{0:T(1024)S(1)} %get-tuple-element.116, f32[704]{0:T(1024)S(1)} %get-tuple-element.69, f32[704]{0:T(1024)S(1)} %get-tuple-element.70, f32[704]{0:T(1024)S(1)} %get-tuple-element.71, ...), kind=kLoop, calls=%fused_computation.336 | loop fusion | flops 35323392 | bytes 3023616 | tf_op jit(solution)/shard_map/reduce_sum | solution.py:36
  24.9 11.3 %psum.56 = f32[512]{0:T(512)S(1)} all-reduce(f32[512]{0:T(512)S(1)} %reduce_sum.512), channel_id=1, replica_groups=mesh['dp'=8,'chan'=4] {'chan'}, use_global_device_ids=true, to_apply=%region_1.2 | all-reduce | flops 512 | bytes 4096 | tf_op jit(solution)/shard_map/psum | solution.py:36
  36.7 8.0 psum.57
  44.7 1.9 copy.71
  49.6 40.4 %all-gather.5.cloned.1.call-done = bf16[512,2816]{0,1:T(8,128)(2,1)} async-done(((bf16[512,704]{0,1:T(8,128)(2,1)}), bf16[512,2816]{0,1:T(8,128)(2,1)}) %all-gather.5.cloned.1.call-update) | async-done | bytes 2883600 | tf_op jit(solution)/shard_map/all_gather | solution.py:42
  90.0 145.3 %all-gather.7.cloned.1.call-done = bf16[2816,2816]{1,0:T(8,128)(2,1)} async-done(((bf16[352,2816]{1,0:T(8,128)(2,1)}), bf16[2816,2816]{1,0:T(8,128)(2,1)}) %all-gather.7.cloned.1.call-update) | async-done | bytes 15859728 | tf_op jit(solution)/shard_map/all_gather | solution.py:43
  235.3 15.1 %fusion.115 = f32[512,2816]{1,0:T(8,128)} fusion(bf16[512,2816]{0,1:T(8,128)(2,1)} %all-gather.5.cloned.1.call-done, bf16[2816,2816]{1,0:T(8,128)(2,1)} %all-gather.7.cloned.1.call-done), kind=kOutput, calls=%fused_computation.337 | convolution fusion | flops 8120172544 | bytes 24510464 | tf_op jit(solution)/shard_map/dot_general | solution.py:44
  250.3 128.5 %all-gather.9.cloned.1.call-done = bf16[2816,2816]{0,1:T(8,128)(2,1)} async-done(((bf16[2816,352]{0,1:T(8,128)(2,1)}), bf16[2816,2816]{0,1:T(8,128)(2,1)}) %all-gather.9.cloned.1.call-update) | async-done | bytes 15859728 | tf_op jit(solution)/shard_map/all_gather | solution.py:46
  378.8 16.3 %convolution_convert_fusion.3 = bf16[512,2816]{0,1:T(8,128)(2,1)} fusion(bf16[2816,2816]{0,1:T(8,128)(2,1)} %all-gather.9.cloned.1.call-done, f32[512,2816]{1,0:T(8,128)} %fusion.115), kind=kOutput, calls=%fused_computation.108 | convolution fusion | flops 8128823296 | bytes 24510464 | tf_op jit(solution)/shard_map/dot_general | solution.py:47
  395.1 2.5 copy.74
  399.3 36.0 %reduce-scatter.5.cloned.1.call-done = bf16[512,704]{0,1:T(8,128)(2,1)} async-done(((bf16[512,2816]{0,1:T(8,128)(2,1)}), bf16[512,704]{0,1:T(8,128)(2,1)}) %reduce-scatter.5.cloned.1.call-update) | async-done | bytes 720912 | tf_op jit(solution)/shard_map/reduce_scatter | solution.py:48
  435.3 3.5 fusion.109
  439.4 41.4 %all-gather.11.cloned.1.call-done = bf16[512,2816]{0,1:T(8,128)(2,1)} async-done(((bf16[512,704]{0,1:T(8,128)(2,1)}), bf16[512,2816]{0,1:T(8,128)(2,1)}) %all-gather.11.cloned.1.call-update) | async-done | bytes 2883600 | tf_op jit(solution)/shard_map/all_gather | solution.py:56
  480.7 16.0 %fusion.5 = bf16[512,2816]{1,0:T(8,128)(2,1)S(1)} fusion(f32[512,2816]{1,0:T(8,128)} %fusion.115, bf16[512,2816]{0,1:T(8,128)(2,1)} %all-gather.11.cloned.1.call-done, bf16[2816,2816]{0,1:T(8,128)(2,1)} %all-gather.9.cloned.1.call-done), kind=kOutput, calls=%fused_computation.104 | convolution fusion | flops 8134590464 | bytes 27394048 | tf_op jit(solution)/shard_map/dot_general | solution.py:57
  498.3 13.0 %convolution_convert_fusion.2 = bf16[512,2816]{0,1:T(8,128)(2,1)} fusion(bf16[512,2816]{1,0:T(8,128)(2,1)S(1)} %fusion.5, bf16[2816,2816]{1,0:T(8,128)(2,1)} %all-gather.7.cloned.1.call-done), kind=kOutput, calls=%fused_computation.107 | convolution fusion | flops 8121614336 | bytes 21626880 | tf_op jit(solution)/shard_map/dot_general | solution.py:71
  511.4 41.9 %reduce-scatter.7.cloned.1.call-done = bf16[512,704]{0,1:T(8,128)(2,1)} async-done(((bf16[512,2816]{0,1:T(8,128)(2,1)}), bf16[512,704]{0,1:T(8,128)(2,1)}) %reduce-scatter.7.cloned.1.call-update) | async-done | bytes 720912 | tf_op jit(solution)/shard_map/reduce_scatter | solution.py:74
  553.3 1.7 fusion.113
  555.0 9.1 all-reduce.2
  564.1 2.6 fusion.111
  566.8 1.8 copy.75
  568.6 3.8 multiply_reduce_fusion.2
  572.4 4.2 multiply_reduce_fusion
  576.7 4.5 multiply_reduce_fusion.1
  582.9 15.4 %convolution_convert_fusion = bf16[2816,2816]{1,0:T(8,128)(2,1)} fusion(bf16[512,2816]{0,1:T(8,128)(2,1)} %all-gather.11.cloned.1.call-done, f32[512,2816]{1,0:T(8,128)} %fusion.115), kind=kOutput, calls=%fused_computation.96 | convolution fusion | flops 8135311360 | bytes 24510464 | tf_op jit(solution)/shard_map/dot_general | solution.py:80
  598.6 13.9 %convolution_convert_fusion.1 = bf16[2816,2816]{1,0:T(8,128)(2,1)} fusion(bf16[512,2816]{0,1:T(8,128)(2,1)} %all-gather.5.cloned.1.call-done, bf16[512,2816]{1,0:T(8,128)(2,1)} %copy-done.7), kind=kOutput, calls=%fused_computation.97 | convolution fusion | flops 8128102400 | bytes 21626880 | tf_op jit(solution)/shard_map/dot_general | solution.py:64
  612.6 2.4 copy.73
  615.2 14.6 %all-reduce.3 = (bf16[704]{0:T(1024)(128)(2,1)S(1)}, bf16[704]{0:T(1024)(128)(2,1)S(1)}, bf16[704]{0:T(1024)(128)(2,1)S(1)}) all-reduce(bf16[704]{0:T(1024)(128)(2,1)S(1)} %get-tuple-element.64, bf16[704]{0:T(1024)(128)(2,1)S(1)} %reduce_sum.567, bf16[704]{0:T(1024)(128)(2,1)S(1)} %get-tuple-element.124), channel_id=1, replica_groups=mesh['dp'=8,'chan'=4] {'dp'}, use_global_device_ids=true, to_apply=%region_61.62 | all-reduce | flops 2112 | bytes 8448 | tf_op jit(solution)/shard_map/psum | solution.py:124
  631.6 12.3 %fusion.102 = bf16[2,16,16,704]{3,2,1,0:T(8,128)(2,1)} fusion(f32[2,16,16,704]{3,2,1,0:T(8,128)S(1)} %bitcast.82, f32[704]{0:T(1024)S(1)} %get-tuple-element.115, f32[704]{0:T(1024)S(1)} %get-tuple-element.116, f32[704]{0:T(1024)S(1)} %get-tuple-element.69, f32[704]{0:T(1024)S(1)} %get-tuple-element.70, f32[704]{0:T(1024)S(1)} %get-tuple-element.71, ...), kind=kLoop, calls=%fused_computation.210 | loop fusion | flops 36044800 | bytes 3021568 | tf_op jit(solution)/shard_map/convert_element_type | solution.py:121
  645.5 152.7 %reduce-scatter.11.cloned.1.call-done = bf16[352,2816]{1,0:T(8,128)(2,1)} async-done(((bf16[2816,2816]{1,0:T(8,128)(2,1)}), bf16[352,2816]{1,0:T(8,128)(2,1)}) %reduce-scatter.11.cloned.1.call-update) | async-done | bytes 1982480 | tf_op jit(solution)/shard_map/reduce_scatter | solution.py:79
  798.2 3.7 convert_bitcast_fusion
  801.9 156.8 %reduce-scatter.9.cloned.1.call-done = bf16[352,2816]{1,0:T(8,128)(2,1)} async-done(((bf16[2816,2816]{1,0:T(8,128)(2,1)}), bf16[352,2816]{1,0:T(8,128)(2,1)}) %reduce-scatter.9.cloned.1.call-update) | async-done | bytes 1982480 | tf_op jit(solution)/shard_map/reduce_scatter | solution.py:63
  958.7 3.7 convert_element_type.88
  (116 shorter events, 17.9 us)
Async XLA Ops:
  7.2 82.8 %all-gather.5.cloned.1.call-start = ((), (), s32[]{:S(2)}) async-start(), calls=%async_computation.4 | async-start | bytes 3604480 | tf_op jit(solution)/shard_map/all_gather | solution.py:42
  24.8 19.9 %copy-start = (f32[2,16,16,704]{3,2,1,0:T(8,128)}, f32[2,16,16,704]{3,2,1,0:T(8,128)S(1)}, u32[]{:S(2)}) copy-start(f32[2,16,16,704]{3,2,1,0:T(8,128)S(1)} %get-tuple-element.123) | copy-start | bytes 4325380
  36.6 9.9 %copy-start.4 = (f32[704]{0:T(1024)S(1)}, f32[704]{0:T(1024)}, u32[]{:S(2)}) copy-start(f32[704]{0:T(1024)} %param.10) | copy-start | bytes 8452
  36.6 9.9 %copy-start.5 = (f32[704]{0:T(1024)S(1)}, f32[704]{0:T(1024)}, u32[]{:S(2)}) copy-start(f32[704]{0:T(1024)} %param.11) | copy-start | bytes 8452
  47.7 187.5 %all-gather.7.cloned.1.call-start = ((), (), s32[]{:S(2)}) async-start(), calls=%async_computation.5 | async-start | bytes 17842176 | tf_op jit(solution)/shard_map/all_gather | solution.py:43
  48.5 330.3 %all-gather.9.cloned.1.call-start = ((), (), s32[]{:S(2)}) async-start(), calls=%async_computation.6 | async-start | bytes 17842176 | tf_op jit(solution)/shard_map/all_gather | solution.py:46
  49.2 386.0 %reduce-scatter.5.cloned.1.call-start = ((), (), s32[]{:S(2)}) async-start(), calls=%async_computation.7 | async-start | bytes 3604480 | tf_op jit(solution)/shard_map/reduce_scatter | solution.py:48
  395.1 85.6 %all-gather.11.cloned.1.call-start = ((), (), s32[]{:S(2)}) async-start(), calls=%async_computation.8 | async-start | bytes 3604480 | tf_op jit(solution)/shard_map/all_gather | solution.py:56
  397.6 37.6 %copy-start.6 = (f32[704]{0:T(1024)S(1)}, f32[704]{0:T(1024)}, u32[]{:S(2)}) copy-start(f32[704]{0:T(1024)} %param.14) | copy-start | bytes 8452
  438.8 114.5 %reduce-scatter.7.cloned.1.call-start = ((), (), s32[]{:S(2)}) async-start(), calls=%async_computation.9 | async-start | bytes 3604480 | tf_op jit(solution)/shard_map/reduce_scatter | solution.py:74
  496.8 1.6 copy-start.7
  511.4 132.5 %all-reduce.6.cloned.1.call-start = ((), (), s32[]{:S(2)}) async-start(), calls=%async_computation.10 | async-start | bytes 172032 | tf_op jit(solution)/shard_map/psum | solution.py:123
  582.2 0.6 copy-start.3
  582.9 215.3 %reduce-scatter.11.cloned.1.call-start = ((), (), s32[]{:S(2)}) async-start(), calls=%async_computation.12 | async-start | bytes 17842176 | tf_op jit(solution)/shard_map/reduce_scatter | solution.py:79
  598.4 360.3 %reduce-scatter.9.cloned.1.call-start = ((), (), s32[]{:S(2)}) async-start(), calls=%async_computation.11 | async-start | bytes 17842176 | tf_op jit(solution)/shard_map/reduce_scatter | solution.py:63
  612.6 2.4 copy-start.1
  612.6 19.0 %copy-start.2 = (bf16[2,16,16,704]{3,2,1,0:T(8,128)(2,1)S(1)}, bf16[2,16,16,704]{3,2,1,0:T(8,128)(2,1)}, u32[]{:S(2)}) copy-start(bf16[2,16,16,704]{3,2,1,0:T(8,128)(2,1)} %param.15) | copy-start | bytes 2162692
Sparse Core Ops, SparseCore 0:
  47.9 42.1 all-gather.4
  91.7 143.5 all-gather.6
  236.9 141.8 all-gather.8
  395.2 39.9 reduce-scatter.4
  438.9 41.7 all-gather.10
  511.5 41.7 reduce-scatter.6
  583.0 49.9 all-reduce.5
  635.5 162.6 reduce-scatter.10
  800.7 157.9 reduce-scatter.8
where the time goes:
time: 974 us; the launch traced here: 969 us
  waiting for transfers between devices  744 us (76%)
  matrix products  89.7 us (9%)
  other arithmetic  58.8 us (6%)
  blocking collectives  43 us (4%)
  local copies, waits for them, and re-layouts  17.3 us (2%)
  between operations  14.7 us (2%)
    reduce_scatter x1, waiting for transfers between devices, body(): lax.psum_scatter(lax.dot_general(columns, dpre, (((0,), (0,)), ((), ())),...  157 us
    reduce_scatter x1, waiting for transfers between devices, body(): lax.psum_scatter(lax.dot_general(columns, hidden, (((0,), (0,)), ((), ())...  153 us
    all_gather x1, waiting for transfers between devices, body(): expand_all = lax.all_gather(w_expand, 'dp', axis=0, tiled=True)  145 us
    all_gather x1, waiting for transfers between devices, body(): reduce_all = lax.all_gather(w_reduce, 'dp', axis=1, tiled=True)  128 us
    reduce_scatter x1, waiting for transfers between devices, body(): lax.psum_scatter(partial_normed.astype(jnp.bfloat16), 'chan', scatter_dim...  41.9 us
    all_gather x1, waiting for transfers between devices, body(): dbranch_all = lax.all_gather(dbranch, 'chan', axis=1, tiled=True)  41.4 us
    all_gather x1, waiting for transfers between devices, body(): normed_all = lax.all_gather(normed_output, 'chan', axis=1, tiled=True)  40.4 us
    reduce_scatter x1, waiting for transfers between devices, body(): lax.psum_scatter(partial_branch.astype(jnp.bfloat16), 'chan', scatter_dim...  36 us
  transfers between devices with their start and end apart: 9, of which 8 were waited for; matrix products, arithmetic and copies ran while one was open for 7% of the time, Pallas kernels for 0%

commit v1 on v0

--- a/solution.py
+++ b/solution.py
@@ -5,6 +5,18 @@
 from jax.sharding import PartitionSpec as P
 
 eps = 1e-06
+
+
+def doubled_up(x, axis, dim):
+    ways, here = (lax.axis_size(axis), lax.axis_index(axis))
+    grown, reach = (x, 1)
+    while reach < ways:
+        theirs = lax.ppermute(grown, axis, [(d, d ^ reach) for d in range(ways)])
+        mine_first = jnp.concatenate([grown, theirs], axis=dim)
+        theirs_first = jnp.concatenate([theirs, grown], axis=dim)
+        grown = jnp.where(here & reach == 0, mine_first, theirs_first)
+        reach = 2 * reach
+    return grown
 
 
 def depthwise(field, kern):
@@ -39,7 +51,7 @@
     inverse_deviation = lax.rsqrt(var + eps)
     standardized_input = centred_rows * inverse_deviation
     normed_output = (standardized_input * layernorm_gain + layernorm_bias).astype(jnp.bfloat16)
-    normed_all = lax.all_gather(normed_output, "chan", axis=1, tiled=True)
+    normed_all = doubled_up(normed_output, "chan", 1)
     expand_all = lax.all_gather(w_expand, "dp", axis=0, tiled=True)
     pre = jnp.dot(normed_all, expand_all, preferred_element_type=jnp.float32)
     hidden = (pre * normal_cdf(pre)).astype(jnp.bfloat16)

time: 974 us -> 894 us (0.918)
  waiting for transfers between devices: 744 us -> 660 us
    all_gather x1, waiting for transfers between devices: 145 us -> 61 us  [body(): expand_all = lax.all_gather(w_expand, 'dp', axis=0, tiled=True)]
    ppermute x0 -> x2, waiting for transfers between devices: none -> 44 us  [doubled_up(): theirs = lax.ppermute(grown, axis, [(d, d ^ reach) for d in range(ways)])]
    all_gather x1 -> x0, waiting for transfers between devices: 40.4 us -> none  [body(): normed_all = lax.all_gather(normed_output, 'chan', axis=1, tiled=True)]
  transfers between devices with their start and end apart: 9 -> 10, of which waited for: 8 -> 9; matrix products, arithmetic and copies ran while one was open for 7% -> 11% of each run, Pallas kernels for 0% -> 0%
where the time goes in v1:
time: 894 us; the launch traced here: 890 us
  waiting for transfers between devices  660 us (74%)
  matrix products  93.7 us (10%)
  other arithmetic  61 us (7%)
  blocking collectives  43.3 us (5%)
  between operations  15 us (2%)
  local copies, waits for them, and re-layouts  14.4 us (2%)
    reduce_scatter x1, waiting for transfers between devices, body(): lax.psum_scatter(lax.dot_general(columns, dpre, (((0,), (0,)), ((), ())),...  157 us
    reduce_scatter x1, waiting for transfers between devices, body(): lax.psum_scatter(lax.dot_general(columns, hidden, (((0,), (0,)), ((), ())...  150 us
    all_gather x1, waiting for transfers between devices, body(): reduce_all = lax.all_gather(w_reduce, 'dp', axis=1, tiled=True)  127 us
    all_gather x1, waiting for transfers between devices, body(): expand_all = lax.all_gather(w_expand, 'dp', axis=0, tiled=True)  61 us
    ppermute x2, waiting for transfers between devices, doubled_up(): theirs = lax.ppermute(grown, axis, [(d, d ^ reach) for d in range(ways)])  44 us
    reduce_scatter x1, waiting for transfers between devices, body(): lax.psum_scatter(partial_normed.astype(jnp.bfloat16), 'chan', scatter_dim...  41.9 us
    all_gather x1, waiting for transfers between devices, body(): dbranch_all = lax.all_gather(dbranch, 'chan', axis=1, tiled=True)  41.4 us
    reduce_scatter x1, waiting for transfers between devices, body(): lax.psum_scatter(partial_branch.astype(jnp.bfloat16), 'chan', scatter_dim...  36 us
  transfers between devices with their start and end apart: 10, of which 9 were waited for; matrix products, arithmetic and copies ran while one was open for 11% of the time, Pallas kernels for 0%

profile of v1, /device:TPU:0, one launch (start us, length us, event | category | flops | bytes accessed | tf_op | source)
XLA Modules:
  0.0 890.2 jit_solution(1510450923336707750)
XLA Ops:
  10.0 12.3 %fusion.117 = (f32[2,16,16]{2,1,0:T(8,128)S(1)}, f32[2,16,16,704]{3,2,1,0:T(8,128)S(1)}) fusion(f32[704]{0:T(1024)S(1)} %get-tuple-element.115, f32[704]{0:T(1024)S(1)} %get-tuple-element.116, f32[704]{0:T(1024)S(1)} %get-tuple-element.69, f32[704]{0:T(1024)S(1)} %get-tuple-element.70, f32[704]{0:T(1024)S(1)} %get-tuple-element.71, ...), kind=kLoop, calls=%fused_computation.341 | loop fusion | flops 35323392 | bytes 3023616 | tf_op jit(solution)/shard_map/reduce_sum | solution.py:48
  22.4 11.3 %psum.56 = f32[512]{0:T(512)S(1)} all-reduce(f32[512]{0:T(512)S(1)} %reduce_sum.512), channel_id=1, replica_groups=mesh['dp'=8,'chan'=4] {'chan'}, use_global_device_ids=true, to_apply=%region_1.2 | all-reduce | flops 512 | bytes 4096 | tf_op jit(solution)/shard_map/psum | solution.py:48
  34.3 1.9 copy.71
  36.1 8.3 psum.57
  47.0 14.3 %collective-permute-done = bf16[512,704]{0,1:T(8,128)(2,1)} collective-permute-done((bf16[512,704]{0,1:T(8,128)(2,1)}, bf16[512,704]{0,1:T(8,128)(2,1)}, u32[]{:S(2)}, u32[]{:S(2)}) %collective-permute-start) | collective-permute-done | bytes 720928 | tf_op jit(solution)/shard_map/ppermute | solution.py:14
  61.3 3.4 maximum_select_fusion.1
  65.3 29.7 %collective-permute-done.1 = bf16[512,1408]{0,1:T(8,128)(2,1)} collective-permute-done((bf16[512,1408]{0,1:T(8,128)(2,1)}, bf16[512,1408]{0,1:T(8,128)(2,1)}, u32[]{:S(2)}, u32[]{:S(2)}) %collective-permute-start.1) | collective-permute-done | bytes 1441824 | tf_op jit(solution)/shard_map/ppermute | solution.py:14
  95.0 61.0 %all-gather.4.cloned.1.call-done = bf16[2816,2816]{1,0:T(8,128)(2,1)} async-done(((bf16[352,2816]{1,0:T(8,128)(2,1)}), bf16[2816,2816]{1,0:T(8,128)(2,1)}) %all-gather.4.cloned.1.call-update) | async-done | bytes 15859728 | tf_op jit(solution)/shard_map/all_gather | solution.py:55
  156.0 16.7 %fusion.114 = f32[512,2816]{1,0:T(8,128)} fusion(bf16[2816,2816]{1,0:T(8,128)(2,1)} %all-gather.4.cloned.1.call-done, bf16[512,1408]{0,1:T(8,128)(2,1)} %collective-permute-done.1, bf16[512,1408]{0,1:T(8,128)(2,1)} %maximum_select_fusion.1, pred[]{:T(512)S(6)} %eq.6), kind=kOutput, calls=%fused_computation.278 | convolution fusion | flops 8133148672 | bytes 24510464 | tf_op jit(solution)/shard_map/dot_general | solution.py:56
  172.7 126.8 %all-gather.6.cloned.1.call-done = bf16[2816,2816]{0,1:T(8,128)(2,1)} async-done(((bf16[2816,352]{0,1:T(8,128)(2,1)}), bf16[2816,2816]{0,1:T(8,128)(2,1)}) %all-gather.6.cloned.1.call-update) | async-done | bytes 15859728 | tf_op jit(solution)/shard_map/all_gather | solution.py:58
  299.5 16.3 %convolution_convert_fusion.3 = bf16[512,2816]{0,1:T(8,128)(2,1)} fusion(bf16[2816,2816]{0,1:T(8,128)(2,1)} %all-gather.6.cloned.1.call-done, f32[512,2816]{1,0:T(8,128)} %fusion.114), kind=kOutput, calls=%fused_computation.108 | convolution fusion | flops 8128823296 | bytes 24510464 | tf_op jit(solution)/shard_map/dot_general | solution.py:59
  315.8 2.5 copy.74
  319.9 36.0 %reduce-scatter.5.cloned.1.call-done = bf16[512,704]{0,1:T(8,128)(2,1)} async-done(((bf16[512,2816]{0,1:T(8,128)(2,1)}), bf16[512,704]{0,1:T(8,128)(2,1)}) %reduce-scatter.5.cloned.1.call-update) | async-done | bytes 720912 | tf_op jit(solution)/shard_map/reduce_scatter | solution.py:60
  355.9 3.5 fusion.109
  360.0 41.4 %all-gather.8.cloned.1.call-done = bf16[512,2816]{0,1:T(8,128)(2,1)} async-done(((bf16[512,704]{0,1:T(8,128)(2,1)}), bf16[512,2816]{0,1:T(8,128)(2,1)}) %all-gather.8.cloned.1.call-update) | async-done | bytes 2883600 | tf_op jit(solution)/shard_map/all_gather | solution.py:68
  401.4 16.0 %fusion.5 = bf16[512,2816]{1,0:T(8,128)(2,1)S(1)} fusion(f32[512,2816]{1,0:T(8,128)} %fusion.114, bf16[512,2816]{0,1:T(8,128)(2,1)} %all-gather.8.cloned.1.call-done, bf16[2816,2816]{0,1:T(8,128)(2,1)} %all-gather.6.cloned.1.call-done), kind=kOutput, calls=%fused_computation.104 | convolution fusion | flops 8134590464 | bytes 27394048 | tf_op jit(solution)/shard_map/dot_general | solution.py:69
  419.0 13.0 %convolution_convert_fusion.2 = bf16[512,2816]{0,1:T(8,128)(2,1)} fusion(bf16[512,2816]{1,0:T(8,128)(2,1)S(1)} %fusion.5, bf16[2816,2816]{1,0:T(8,128)(2,1)} %all-gather.4.cloned.1.call-done), kind=kOutput, calls=%fused_computation.107 | convolution fusion | flops 8121614336 | bytes 21626880 | tf_op jit(solution)/shard_map/dot_general | solution.py:83
  432.1 41.9 %reduce-scatter.7.cloned.1.call-done = bf16[512,704]{0,1:T(8,128)(2,1)} async-done(((bf16[512,2816]{0,1:T(8,128)(2,1)}), bf16[512,704]{0,1:T(8,128)(2,1)}) %reduce-scatter.7.cloned.1.call-update) | async-done | bytes 720912 | tf_op jit(solution)/shard_map/reduce_scatter | solution.py:86
  475.7 9.1 %all-reduce.2 = (f32[512]{0:T(512)S(1)}, f32[512]{0:T(512)S(1)}) all-reduce(f32[512]{0:T(512)S(1)} %get-tuple-element.65, f32[512]{0:T(512)S(1)} %get-tuple-element.67), channel_id=1, replica_groups=mesh['dp'=8,'chan'=4] {'chan'}, use_global_device_ids=true, to_apply=%region_9.10 | all-reduce | flops 1024 | bytes 8192 | tf_op jit(solution)/shard_map/psum | solution.py:105
  484.8 2.6 fusion.111
  489.3 3.8 multiply_reduce_fusion.2
  493.1 4.2 multiply_reduce_fusion
  497.3 4.5 multiply_reduce_fusion.1
  503.6 15.4 %convolution_convert_fusion = bf16[2816,2816]{1,0:T(8,128)(2,1)} fusion(bf16[512,2816]{0,1:T(8,128)(2,1)} %all-gather.8.cloned.1.call-done, f32[512,2816]{1,0:T(8,128)} %fusion.114), kind=kOutput, calls=%fused_computation.96 | convolution fusion | flops 8135311360 | bytes 24510464 | tf_op jit(solution)/shard_map/dot_general | solution.py:92
  519.3 16.2 %convolution_convert_fusion.1 = bf16[2816,2816]{1,0:T(8,128)(2,1)} fusion(bf16[512,2816]{1,0:T(8,128)(2,1)} %copy-done.9, bf16[512,1408]{0,1:T(8,128)(2,1)} %collective-permute-done.1, bf16[512,1408]{0,1:T(8,128)(2,1)} %maximum_select_fusion.1, pred[]{:T(512)S(6)} %eq.6), kind=kOutput, calls=%fused_computation.97 | convolution fusion | flops 8141078528 | bytes 21626880 | tf_op jit(solution)/shard_map/dot_general | solution.py:76
  535.5 2.4 copy.73
  538.1 14.6 %all-reduce.3 = (bf16[704]{0:T(1024)(128)(2,1)S(1)}, bf16[704]{0:T(1024)(128)(2,1)S(1)}, bf16[704]{0:T(1024)(128)(2,1)S(1)}) all-reduce(bf16[704]{0:T(1024)(128)(2,1)S(1)} %get-tuple-element.64, bf16[704]{0:T(1024)(128)(2,1)S(1)} %reduce_sum.567, bf16[704]{0:T(1024)(128)(2,1)S(1)} %get-tuple-element.124), channel_id=1, replica_groups=mesh['dp'=8,'chan'=4] {'dp'}, use_global_device_ids=true, to_apply=%region_61.62 | all-reduce | flops 2112 | bytes 8448 | tf_op jit(solution)/shard_map/psum | solution.py:136
  554.5 12.3 %fusion.102 = bf16[2,16,16,704]{3,2,1,0:T(8,128)(2,1)} fusion(f32[2,16,16,704]{3,2,1,0:T(8,128)S(1)} %bitcast.80, f32[704]{0:T(1024)S(1)} %get-tuple-element.115, f32[704]{0:T(1024)S(1)} %get-tuple-element.116, f32[704]{0:T(1024)S(1)} %get-tuple-element.69, f32[704]{0:T(1024)S(1)} %get-tuple-element.70, f32[704]{0:T(1024)S(1)} %get-tuple-element.71, ...), kind=kLoop, calls=%fused_computation.211 | loop fusion | flops 36044800 | bytes 3021568 | tf_op jit(solution)/shard_map/convert_element_type | solution.py:133
  568.4 150.5 %reduce-scatter.11.cloned.1.call-done = bf16[352,2816]{1,0:T(8,128)(2,1)} async-done(((bf16[2816,2816]{1,0:T(8,128)(2,1)}), bf16[352,2816]{1,0:T(8,128)(2,1)}) %reduce-scatter.11.cloned.1.call-update) | async-done | bytes 1982480 | tf_op jit(solution)/shard_map/reduce_scatter | solution.py:91
  718.9 3.7 convert_bitcast_fusion
  722.6 156.7 %reduce-scatter.9.cloned.1.call-done = bf16[352,2816]{1,0:T(8,128)(2,1)} async-done(((bf16[2816,2816]{1,0:T(8,128)(2,1)}), bf16[352,2816]{1,0:T(8,128)(2,1)}) %reduce-scatter.9.cloned.1.call-update) | async-done | bytes 1982480 | tf_op jit(solution)/shard_map/reduce_scatter | solution.py:75
  879.4 3.7 convert_element_type.88
  (122 shorter events, 19.2 us)
Async XLA Ops:
  7.2 1.6 copy-start.2
  7.2 148.8 %all-gather.4.cloned.1.call-start = ((), (), s32[]{:S(2)}) async-start(), calls=%async_computation.4 | async-start | bytes 17842176 | tf_op jit(solution)/shard_map/all_gather | solution.py:55
  7.9 291.6 %all-gather.6.cloned.1.call-start = ((), (), s32[]{:S(2)}) async-start(), calls=%async_computation.5 | async-start | bytes 17842176 | tf_op jit(solution)/shard_map/all_gather | solution.py:58
  8.7 0.9 copy-start.4
  8.7 347.2 %reduce-scatter.5.cloned.1.call-start = ((), (), s32[]{:S(2)}) async-start(), calls=%async_computation.6 | async-start | bytes 3604480 | tf_op jit(solution)/shard_map/reduce_scatter | solution.py:60
  22.3 11.9 %copy-start = (f32[2,16,16,704]{3,2,1,0:T(8,128)}, f32[2,16,16,704]{3,2,1,0:T(8,128)S(1)}, u32[]{:S(2)}) copy-start(f32[2,16,16,704]{3,2,1,0:T(8,128)S(1)} %get-tuple-element.123) | copy-start | bytes 4325380
  34.2 10.3 %copy-start.6 = (f32[704]{0:T(1024)S(1)}, f32[704]{0:T(1024)}, u32[]{:S(2)}) copy-start(f32[704]{0:T(1024)} %param.10) | copy-start | bytes 8452
  34.2 10.2 %copy-start.7 = (f32[704]{0:T(1024)S(1)}, f32[704]{0:T(1024)}, u32[]{:S(2)}) copy-start(f32[704]{0:T(1024)} %param.11) | copy-start | bytes 8452
  45.6 15.8 %collective-permute-start = (bf16[512,704]{0,1:T(8,128)(2,1)}, bf16[512,704]{0,1:T(8,128)(2,1)}, u32[]{:S(2)}, u32[]{:S(2)}) collective-permute-start(bf16[512,704]{0,1:T(8,128)(2,1)} %add_convert_fusion), channel_id=1, source_target_pairs={{0,1},{1,0},{2,3},{3,2},{4,5},{5,4},{6,7},{7,6},{8,9},{9,8},{10,11... | collective-permute-start | bytes 2162696 | tf_op jit(solution)/shard_map/ppermute | solution.py:14
  64.7 30.3 %collective-permute-start.1 = (bf16[512,1408]{0,1:T(8,128)(2,1)}, bf16[512,1408]{0,1:T(8,128)(2,1)}, u32[]{:S(2)}, u32[]{:S(2)}) collective-permute-start(bf16[512,1408]{0,1:T(8,128)(2,1)} %maximum_select_fusion.1), channel_id=1, source_target_pairs={{0,2},{1,3},{2,0},{3,1},{4,6},{5,7},{6,4},{7,5},{8,10},{9,11},{10,... | collective-permute-start | bytes 4325384 | tf_op jit(solution)/shard_map/ppermute | solution.py:14
  315.8 85.6 %all-gather.8.cloned.1.call-start = ((), (), s32[]{:S(2)}) async-start(), calls=%async_computation.7 | async-start | bytes 3604480 | tf_op jit(solution)/shard_map/all_gather | solution.py:68
  318.3 37.6 %copy-start.8 = (f32[704]{0:T(1024)S(1)}, f32[704]{0:T(1024)}, u32[]{:S(2)}) copy-start(f32[704]{0:T(1024)} %param.14) | copy-start | bytes 8452
  359.4 114.6 %reduce-scatter.7.cloned.1.call-start = ((), (), s32[]{:S(2)}) async-start(), calls=%async_computation.8 | async-start | bytes 3604480 | tf_op jit(solution)/shard_map/reduce_scatter | solution.py:86
  417.4 1.6 copy-start.9
  432.1 134.8 %all-reduce.6.cloned.1.call-start = ((), (), s32[]{:S(2)}) async-start(), calls=%async_computation.9 | async-start | bytes 172032 | tf_op jit(solution)/shard_map/psum | solution.py:135
  502.9 0.6 copy-start.5
  503.5 215.4 %reduce-scatter.11.cloned.1.call-start = ((), (), s32[]{:S(2)}) async-start(), calls=%async_computation.11 | async-start | bytes 17842176 | tf_op jit(solution)/shard_map/reduce_scatter | solution.py:91
  519.0 360.4 %reduce-scatter.9.cloned.1.call-start = ((), (), s32[]{:S(2)}) async-start(), calls=%async_computation.10 | async-start | bytes 17842176 | tf_op jit(solution)/shard_map/reduce_scatter | solution.py:75
  535.5 2.4 copy-start.1
  535.5 19.0 %copy-start.3 = (bf16[2,16,16,704]{3,2,1,0:T(8,128)(2,1)S(1)}, bf16[2,16,16,704]{3,2,1,0:T(8,128)(2,1)}, u32[]{:S(2)}) copy-start(bf16[2,16,16,704]{3,2,1,0:T(8,128)(2,1)} %param.15) | copy-start | bytes 2162692
Sparse Core Ops, SparseCore 0:
  9.7 146.2 all-gather.3
  157.6 141.8 all-gather.5
  315.9 39.9 reduce-scatter.4
  359.5 41.7 all-gather.7
  432.2 41.7 reduce-scatter.6
  503.7 50.0 all-reduce.5
  556.2 162.6 reduce-scatter.10
  721.4 157.9 reduce-scatter.8
